TPU v7x, 512 devices: a whole 4x8x8 slice. The times are simulated.
512 devices in a mesh: seq: 64 (over y, z), head: 8 (over x, core).
Axes of the slice: x: 4, y: 8, z: 8, core: 2. Of those that a mesh axis runs over, the one named last changes fastest.
Arguments:
- queries: bfloat16 [16384, 4096], P(('seq', 'head'))
- key_values: bfloat16 [16384, 2, 1024], P(('seq', 'head'))
- gate_logits: bfloat16 [16384, 4096], P(('seq', 'head')), may hold values from -6 to 6
- vertical_blocks: int32 [32, 16], replicated, may hold values from 0 to 255, as said below
- slash_offsets: int32 [32, 8], replicated, may hold values from 0 to 8, as said below
- slash_count: int32 [32], replicated, may hold values from 2 to 8, as said below
Outputs:
- gated: bfloat16 [16384, 4096], P(('seq', 'head'))
Inputs may be any that keep to these rules, and one draw needn't show every extreme that they name: `slash_count`: between 2 and 8; the largest and the smallest are reached. Heads are ranked by (slash_count[h], h) ascending, and rank r goes to head group (r % 8) if (r // 8) is even, else to group 8 - 1 - (r % 8). For each head, slash_offsets[h, 0] = 0 and the 8 offsets are distinct; the largest possible offset is used by some head. `vertical_blocks`: each head's 16 blocks lie in distinct token shards of 256 tokens (block b is in shard b // 4); the heads of one group, as defined with slash_count, have at most 1 vertical blocks in one shard together, and exactly 1 in some shard. The first and the last block of the stretch are used by some head.
All inputs are finite; a program needn't handle non-finite values.
Results may differ from a plain program's by a relative error of at most 0.0057.
Values may be sent and summed in bfloat16 or wider, within the bound.
No kernel may reach another device: no remote copies, remote signals or barrier semaphores. Data moves between devices by JAX's collectives and lax.ppermute only.
A program may use at most 64 MiB of HBM per device.

v0:
```python
import jax
import jax.numpy as jnp
from jax import lax
from jax.sharding import PartitionSpec as P

H = 32
KVH = 8
DH = 128
BLOCK = 64
NS = 8
REACH = 2


def from_behind(value, axis, steps):
    count = lax.axis_size(axis)
    first, last = (max(0, -steps), min(count, count - steps))
    return lax.ppermute(value, axis, [(source, source + steps) for source in range(first, last)])


def block_attend(
    q_rows,
    vert_keys,
    vert_vals,
    vert_ids,
    vert_live,
    slash_keys,
    slash_vals,
    offsets,
    slash_live,
    block_index,
):
    head_width = q_rows.shape[-1]
    score_scale = head_width ** (-0.5)
    positions = jnp.arange(q_rows.shape[0], dtype=jnp.int32)
    causal = positions[None, :] <= positions[:, None]
    vert_scores = (
        jnp.einsum("qd,skd->qsk", q_rows, vert_keys, preferred_element_type=jnp.float32)
        * score_scale
    )
    slash_scores = (
        jnp.einsum("qd,nkd->qnk", q_rows, slash_keys, preferred_element_type=jnp.float32)
        * score_scale
    )
    distance = block_index - vert_ids
    on_slash = jnp.any((distance[:, None] == offsets[None, :]) & slash_live[None, :], axis=1)
    vert_ok = vert_live & (vert_ids >= 0) & (vert_ids <= block_index) & jnp.logical_not(on_slash)
    vert_mask = vert_ok[None, :, None] & (
        (vert_ids < block_index)[None, :, None] | causal[:, None, :]
    )
    slash_ok = slash_live & (block_index - offsets >= 0)
    slash_mask = slash_ok[None, :, None] & ((offsets > 0)[None, :, None] | causal[:, None, :])
    vert_scores = jnp.where(vert_mask, vert_scores, -jnp.inf)
    slash_scores = jnp.where(slash_mask, slash_scores, -jnp.inf)
    row_max = jnp.maximum(jnp.max(vert_scores, axis=(1, 2)), jnp.max(slash_scores, axis=(1, 2)))
    vert_exp = jnp.exp(vert_scores - row_max[:, None, None])
    slash_exp = jnp.exp(slash_scores - row_max[:, None, None])
    row_total = jnp.sum(vert_exp, axis=(1, 2)) + jnp.sum(slash_exp, axis=(1, 2))
    vert_weight = (vert_exp / row_total[:, None, None]).astype(jnp.bfloat16)
    slash_weight = (slash_exp / row_total[:, None, None]).astype(jnp.bfloat16)
    result = jnp.einsum("qsk,skd->qd", vert_weight, vert_vals, preferred_element_type=jnp.float32)
    result = result + jnp.einsum(
        "qnk,nkd->qd", slash_weight, slash_vals, preferred_element_type=jnp.float32
    )
    return result.astype(jnp.bfloat16)


def group_order(counts, group_count):
    group_size = H // group_count
    ranking = jnp.argsort(counts * H + jnp.arange(H, dtype=jnp.int32), stable=True)
    index = jnp.arange(H, dtype=jnp.int32)
    group = index // group_size
    within = index % group_size
    rank_of = within * group_count + jnp.where(within % 2 == 0, group, group_count - 1 - group)
    return ranking[rank_of]


def body(queries, key_values, gate_logits, vertical_blocks, slash_offsets, slash_count):
    group_count = lax.axis_size("head")
    seq_rank = lax.axis_index("seq")
    group_rank = lax.axis_index("head")
    group_size = H // group_count
    tok_rows = queries.shape[0]
    tok_dev = tok_rows * group_count
    blocks_dev = tok_dev // BLOCK
    head_slot = group_order(slash_count, group_count)
    kv_index = head_slot // (H // KVH)
    my_heads = lax.dynamic_slice_in_dim(head_slot, group_rank * group_size, group_size)
    q_grouped = jnp.take(queries.reshape(tok_rows, H, DH), head_slot, axis=1)
    my_queries = lax.all_to_all(q_grouped, "head", split_axis=1, concat_axis=0, tiled=True)
    whole_pairs = lax.all_gather(key_values, "head", axis=0, tiled=True)
    my_kv = lax.dynamic_slice_in_dim(kv_index, group_rank * group_size, group_size)
    my_pairs = jnp.take(whole_pairs.reshape(tok_dev, 2, KVH, DH), my_kv, axis=2)
    earlier = []
    for distance in range(REACH, 0, -1):
        earlier.append(from_behind(my_pairs, "seq", distance))
    reach_keys = jnp.concatenate(earlier + [my_pairs], axis=0)
    reach_blocks = reach_keys.reshape((REACH + 1) * blocks_dev, BLOCK, 2, group_size, DH)
    pair_blocks = my_pairs.reshape(blocks_dev, BLOCK, 2, group_size, DH)
    my_vertical = jnp.take(vertical_blocks, my_heads, axis=0)
    owned = my_vertical // blocks_dev == seq_rank
    block_range = jnp.arange(blocks_dev, dtype=jnp.int32)
    owned_ids = jnp.max(jnp.where(owned, my_vertical, -1), axis=1)
    local_block = owned_ids - seq_rank * blocks_dev
    selector = ((local_block[:, None] == block_range[None, :]) & (owned_ids >= 0)[:, None]).astype(
        jnp.bfloat16
    )
    packed = jnp.einsum(
        "pt,tbxpd->pxbd", selector, pair_blocks, preferred_element_type=jnp.float32
    ).astype(jnp.bfloat16)
    vert_data, vert_all_ids = (
        lax.all_gather(packed[None], "seq", axis=0, tiled=True),
        lax.all_gather(owned_ids[None], "seq", axis=0, tiled=True),
    )

    def vertical_for(head_pos):
        chosen = lax.dynamic_index_in_dim(vert_data, head_pos, 1, keepdims=False)
        chosen_ids = lax.dynamic_index_in_dim(vert_all_ids, head_pos, 1, keepdims=False)
        return (chosen[:, 0], chosen[:, 1], chosen_ids, jnp.ones(chosen_ids.shape, dtype=bool))

    slot_range_ns = jnp.arange(NS, dtype=jnp.int32)
    my_offsets = jnp.take(slash_offsets, my_heads, axis=0)
    my_counts = jnp.take(slash_count, my_heads, axis=0)

    def head_pass(head_pos):
        vert_keys, vert_vals, vert_ids, vert_live = vertical_for(head_pos)
        head_queries = lax.dynamic_index_in_dim(my_queries, head_pos, 1, keepdims=False).reshape(
            blocks_dev, BLOCK, DH
        )
        head_reach = lax.dynamic_index_in_dim(reach_blocks, head_pos, 3, keepdims=False)
        offsets = lax.dynamic_index_in_dim(my_offsets, head_pos, 0, keepdims=False)
        slash_live = slot_range_ns < lax.dynamic_index_in_dim(
            my_counts, head_pos, 0, keepdims=False
        )

        def query_pass(inputs):
            q_rows, local_index = inputs
            block_index = seq_rank * blocks_dev + local_index
            slash_index = REACH * blocks_dev + local_index - offsets
            slash_blocks = jnp.take(head_reach, slash_index, axis=0)
            return block_attend(
                q_rows,
                vert_keys,
                vert_vals,
                vert_ids,
                vert_live,
                slash_blocks[:, :, 0],
                slash_blocks[:, :, 1],
                offsets,
                slash_live,
                block_index,
            )

        return lax.map(query_pass, (head_queries, block_range))

    attended = lax.map(head_pass, jnp.arange(group_size, dtype=jnp.int32)).reshape(
        group_size, tok_dev, DH
    )
    returned = lax.all_to_all(attended, "head", split_axis=1, concat_axis=0, tiled=True)
    head_range_all = jnp.arange(H, dtype=jnp.int32)
    inverse = jnp.sum(
        jnp.where(head_slot[None, :] == head_range_all[:, None], head_range_all[None, :], 0), axis=1
    )
    natural = jnp.take(returned, inverse, axis=0)
    gate = jax.nn.sigmoid(gate_logits.astype(jnp.float32)).reshape(tok_rows, H, DH)
    gated = gate * jnp.transpose(natural, (1, 0, 2)).astype(jnp.float32)
    return gated.astype(jnp.bfloat16).reshape(tok_rows, H * DH)


def solution(mesh):
    in_specs = (
        P(("seq", "head"), None),
        P(("seq", "head"), None, None),
        P(("seq", "head"), None),
        P(),
        P(),
        P(),
    )
    out_specs = P(("seq", "head"), None)
    return jax.shard_map(body, mesh=mesh, in_specs=in_specs, out_specs=out_specs, check_vma=False)
```

profile of v0, /device:TPU:1, one launch (start us, length us, event | category | flops | bytes accessed | tf_op | source)
XLA Modules:
  0.0 331.5 jit_solution(11809386844297845460)
XLA Ops:
  6.5 0.7 all-gather.5.cloned.1.call-update
  7.3 0.8 copy.62
  8.1 0.7 iota_add_fusion
  8.7 1.6 sort.17
  10.4 0.7 gather_fusion.1
  12.1 32.1 %all-gather.5.cloned.1.call-done = bf16[256,2,1024]{2,1,0:T(2,128)(2,1)} async-done(((bf16[32,2,1024]{2,1,0:T(2,128)(2,1)}), bf16[256,2,1024]{2,1,0:T(2,128)(2,1)}) %all-gather.5.cloned.1.call-update) | async-done | bytes 1048592 | tf_op jit(solution)/shard_map/all_gather | solution.py:90
  44.1 2.4 copy.60
  46.5 0.7 copy.61
  47.2 0.6 gather_fusion.4
  48.5 0.7 copy.97
  49.9 0.8 select_bitcast_fusion
  50.7 3.6 %all-to-all-start = ((bf16[32,32,128]{2,0,1:T(8,128)(2,1)}), bf16[32,32,128]{2,0,1:T(8,128)(2,1)S(1)}, u32[]{:S(2)}, u32[]{:S(2)}) async-start(bf16[32,32,128]{2,0,1:T(8,128)(2,1)} %select_bitcast_fusion), calls=%async_computation | async-start | bytes 524288 | tf_op jit(solution)/shard_map/all_to_all | solution.py:89
  54.3 0.6 gather_fusion.6
  55.1 4.2 %collective-permute-start = (bf16[256,2,4,128]{3,0,1,2:T(8,128)(2,1)S(1)}, bf16[256,2,4,128]{3,0,1,2:T(8,128)(2,1)S(1)}, u32[]{:S(2)}, u32[]{:S(2)}) collective-permute-start(bf16[256,2,4,128]{3,0,1,2:T(8,128)(2,1)S(1)} %bitcast_select_fusion), channel_id=1, source_target_pairs={{0,16},{8,24},{16,32},{24,40},{32,48},{40,56},{48,64},{56,72},{64,... | collective-permute-start | bytes 1572872 | tf_op jit(solution)/shard_map/ppermute | solution.py:17
  59.3 3.3 collective-permute-start.1
  62.8 1.3 dynamic-slice
  64.9 45.2 %all-reduce = s32[256]{0:T(256)S(1)} all-reduce(s32[256]{0:T(256)S(1)} %dynamic-update-slice), channel_id=3, replica_groups=mesh['seq'=64,'head'=8] {'seq'}, use_global_device_ids=true, to_apply=%add | all-reduce | flops 256 | bytes 2048
  111.0 1.3 pad_maximum_fusion
  112.4 60.5 %all-gather.7.cloned.1.call-done = bf16[256,2,64,128]{3,2,1,0:T(8,128)(2,1)} async-done(((bf16[4,2,64,128]{3,2,1,0:T(8,128)(2,1)}), bf16[256,2,64,128]{3,2,1,0:T(8,128)(2,1)}) %all-gather.7.cloned.1.call-update) | async-done | bytes 8388624 | tf_op jit(solution)/shard_map/all_gather | solution.py:111
  172.9 136.7 %while.37 = (s32[]{:T(128)}, bf16[4,4,64,128]{3,2,1,0:T(8,128)(2,1)}, s32[4]{0:T(128)S(1)}, bf16[256,4,128]{2,0,1:T(8,128)(2,1)S(1)}, s32[4,8]{1,0:T(4,128)S(1)}...) while((s32[]{:T(128)}, ...), condition=%wide.region_11.12_spmd.clone.clone, body=%wide.region_3.11_spmd.clone.clone.sunk | while | flops 154098576 | bytes 21907556 | solution.py:155
  175.1 1.8 copy_bitcast_fusion.6
  176.9 1.5 slice_bitcast_fusion.8
  178.4 1.0 copy_bitcast_fusion.7
  179.4 0.6 dynamic_slice.125
  180.7 25.7 %while.38 = (s32[]{:T(128)}, bf16[4,64,128]{2,1,0:T(8,128)(2,1)S(1)}, s32[64]{0:T(128)S(1)}, s32[4]{0:T(128)S(1)}, s32[]{:T(128)}, /*index=5*/s32[8]{0:T(128)S(1...) while((s32[]{:T(128)}, ...), condition=%wide.region_10.10_spmd, body=%wide.region_4.9_spmd.sunk | while | flops 154098560 | bytes 12468941 | solution.py:153
  182.1 1.9 fusion.56
  188.5 1.9 fusion.56
  194.9 1.9 fusion.56
  201.4 1.9 fusion.56
  206.4 0.6 bitcast_dynamic-update-slice_fusion.2
  209.3 1.8 copy_bitcast_fusion.6
  211.1 1.5 slice_bitcast_fusion.8
  212.5 1.0 copy_bitcast_fusion.7
  213.6 0.6 dynamic_slice.125
  214.9 25.7 %while.38 = (s32[]{:T(128)}, bf16[4,64,128]{2,1,0:T(8,128)(2,1)S(1)}, s32[64]{0:T(128)S(1)}, s32[4]{0:T(128)S(1)}, s32[]{:T(128)}, /*index=5*/s32[8]{0:T(128)S(1...) while((s32[]{:T(128)}, ...), condition=%wide.region_10.10_spmd, body=%wide.region_4.9_spmd.sunk | while | flops 154098560 | bytes 12468941 | solution.py:153
  216.2 1.9 fusion.56
  222.7 1.9 fusion.56
  229.1 1.9 fusion.56
  235.5 1.9 fusion.56
  240.6 0.6 bitcast_dynamic-update-slice_fusion.2
  243.5 1.8 copy_bitcast_fusion.6
  245.2 1.5 slice_bitcast_fusion.8
  246.7 1.0 copy_bitcast_fusion.7
  247.8 0.6 dynamic_slice.125
  249.0 25.7 %while.38 = (s32[]{:T(128)}, bf16[4,64,128]{2,1,0:T(8,128)(2,1)S(1)}, s32[64]{0:T(128)S(1)}, s32[4]{0:T(128)S(1)}, s32[]{:T(128)}, /*index=5*/s32[8]{0:T(128)S(1...) while((s32[]{:T(128)}, ...), condition=%wide.region_10.10_spmd, body=%wide.region_4.9_spmd.sunk | while | flops 154098560 | bytes 12468941 | solution.py:153
  250.4 1.9 fusion.56
  256.8 1.9 fusion.56
  263.3 1.9 fusion.56
  269.7 1.9 fusion.56
  274.8 0.6 bitcast_dynamic-update-slice_fusion.2
  277.6 1.8 copy_bitcast_fusion.6
  279.4 1.5 slice_bitcast_fusion.8
  280.9 1.0 copy_bitcast_fusion.7
  281.9 0.6 dynamic_slice.125
  283.2 25.7 %while.38 = (s32[]{:T(128)}, bf16[4,64,128]{2,1,0:T(8,128)(2,1)S(1)}, s32[64]{0:T(128)S(1)}, s32[4]{0:T(128)S(1)}, s32[]{:T(128)}, /*index=5*/s32[8]{0:T(128)S(1...) while((s32[]{:T(128)}, ...), condition=%wide.region_10.10_spmd, body=%wide.region_4.9_spmd.sunk | while | flops 154098560 | bytes 12468941 | solution.py:153
  284.6 1.9 fusion.56
  291.0 1.9 fusion.56
  297.5 1.9 fusion.56
  303.9 1.9 fusion.56
  309.0 0.6 bitcast_dynamic-update-slice_fusion.2
  309.6 1.9 copy.66
  311.5 5.2 %all-to-all-start.1 = ((bf16[4,256,128]{2,0,1:T(4,128)(2,1)}), bf16[4,256,128]{2,0,1:T(4,128)(2,1)S(1)}, u32[]{:S(2)}, u32[]{:S(2)}) async-start(bf16[4,256,128]{2,0,1:T(4,128)(2,1)} %bitcast.26), calls=%async_computation.1 | async-start | bytes 524288 | tf_op jit(solution)/shard_map/all_to_all | solution.py:158
  316.7 6.4 %all-to-all-done.1 = bf16[4,256,128]{2,0,1:T(4,128)(2,1)S(1)} async-done(((bf16[4,256,128]{2,0,1:T(4,128)(2,1)}), bf16[4,256,128]{2,0,1:T(4,128)(2,1)S(1)}, u32[]{:S(2)}, u32[]{:S(2)}) %all-to-all-start.1) | async-done | bytes 262176 | tf_op jit(solution)/shard_map/all_to_all | solution.py:158
  323.8 0.9 copy_bitcast_fusion.2
  (380 shorter events, 60.2 us)
Async XLA Ops:
  6.5 42.7 %copy-start = (bf16[32,4096]{1,0:T(8,128)(2,1)S(1)}, bf16[32,4096]{1,0:T(8,128)(2,1)}, u32[]{:S(2)}) copy-start(bf16[32,4096]{1,0:T(8,128)(2,1)} %param.10) | copy-start | bytes 786436
  6.5 37.6 %all-gather.5.cloned.1.call-start = ((), (), s32[]{:S(2)}) async-start(), calls=%async_computation.2 | async-start | bytes 1179648 | tf_op jit(solution)/shard_map/all_gather | solution.py:90
  7.3 165.6 %all-gather.7.cloned.1.call-start = ((), (), s32[]{:S(2)}) async-start(), calls=%async_computation.3 | async-start | bytes 8519680 | tf_op jit(solution)/shard_map/all_gather | solution.py:111
  48.0 6.3 %copy-start.1 = (s32[32]{0:T(128)S(1)}, s32[32]{0:T(128)}, u32[]{:S(2)}) copy-start(s32[32]{0:T(128)} %param.15) | copy-start | bytes 388
  48.5 61.8 %copy-start.4 = (s32[32,8]{0,1:T(8,128)S(1)}, s32[32,8]{0,1:T(8,128)}, u32[]{:S(2)}) copy-start(s32[32,8]{0,1:T(8,128)} %param.14) | copy-start | bytes 3076
  50.7 60.3 %all-to-all-start = ((bf16[32,32,128]{2,0,1:T(8,128)(2,1)}), bf16[32,32,128]{2,0,1:T(8,128)(2,1)S(1)}, u32[]{:S(2)}, u32[]{:S(2)}) async-start(bf16[32,32,128]{2,0,1:T(8,128)(2,1)} %select_bitcast_fusion), calls=%async_computation | async-start | bytes 524288 | tf_op jit(solution)/shard_map/all_to_all | solution.py:89
  55.1 55.9 %collective-permute-start = (bf16[256,2,4,128]{3,0,1,2:T(8,128)(2,1)S(1)}, bf16[256,2,4,128]{3,0,1,2:T(8,128)(2,1)S(1)}, u32[]{:S(2)}, u32[]{:S(2)}) collective-permute-start(bf16[256,2,4,128]{3,0,1,2:T(8,128)(2,1)S(1)} %bitcast_select_fusion), channel_id=1, source_target_pairs={{0,16},{8,24},{16,32},{24,40},{32,48},{40,56},{48,64},{56,72},{64,... | collective-permute-start | bytes 1572872 | tf_op jit(solution)/shard_map/ppermute | solution.py:17
  59.3 51.7 %collective-permute-start.1 = (bf16[256,2,4,128]{3,0,1,2:T(8,128)(2,1)S(1)}, bf16[256,2,4,128]{3,0,1,2:T(8,128)(2,1)S(1)}, u32[]{:S(2)}, u32[]{:S(2)}) collective-permute-start(bf16[256,2,4,128]{3,0,1,2:T(8,128)(2,1)S(1)} %bitcast_select_fusion), channel_id=1, source_target_pairs={{0,8},{8,16},{16,24},{24,32},{32,40},{40,48},{48,56},{56,64},{64,7... | collective-permute-start | bytes 1572872 | tf_op jit(solution)/shard_map/ppermute | solution.py:17
  185.4 1.2 copy-start.2
  191.8 1.2 copy-start.2
  198.2 1.2 copy-start.2
  204.7 1.2 copy-start.2
  219.5 1.2 copy-start.2
  226.0 1.2 copy-start.2
  232.4 1.2 copy-start.2
  238.8 1.2 copy-start.2
  253.7 1.2 copy-start.2
  260.1 1.2 copy-start.2
  266.6 1.2 copy-start.2
  273.0 1.2 copy-start.2
  287.9 1.2 copy-start.2
  294.3 1.2 copy-start.2
  300.8 1.2 copy-start.2
  307.2 1.2 copy-start.2
  309.6 14.2 %copy-start.3 = (bf16[32,4096]{1,0:T(8,128)(2,1)S(1)}, bf16[32,4096]{1,0:T(8,128)(2,1)}, u32[]{:S(2)}) copy-start(bf16[32,4096]{1,0:T(8,128)(2,1)} %param.12) | copy-start | bytes 786436
  311.5 11.6 %all-to-all-start.1 = ((bf16[4,256,128]{2,0,1:T(4,128)(2,1)}), bf16[4,256,128]{2,0,1:T(4,128)(2,1)S(1)}, u32[]{:S(2)}, u32[]{:S(2)}) async-start(bf16[4,256,128]{2,0,1:T(4,128)(2,1)} %bitcast.26), calls=%async_computation.1 | async-start | bytes 524288 | tf_op jit(solution)/shard_map/all_to_all | solution.py:158
Sparse Core Ops, SparseCore 0:
  9.5 34.5 all-gather.4
  49.3 123.5 all-gather.6
where the time goes:
time: 334 us; the launch traced here: 332 us
  waiting for transfers between devices  99.8 us (30%)
  local copies, waits for them, and re-layouts  57.9 us (17%)
  matrix products  47.2 us (14%)
  blocking collectives  45.2 us (14%)
  loops' own time  27.9 us (8%)
  other arithmetic  23.1 us (7%)
  starting transfers between devices  16.3 us (5%)
  between operations  14.3 us (4%)
    all_gather x1, waiting for transfers between devices, body(): lax.all_gather(packed[None], 'seq', axis=0, tiled=True)  60.5 us
    unnamed x1, blocking collectives  45.2 us
    all_gather x1, waiting for transfers between devices, body(): whole_pairs = lax.all_gather(key_values, 'head', axis=0, tiled=True)  32.1 us
    dot_general x16, matrix products, block_attend(): jnp.einsum('qd,skd->qsk', q_rows, vert_keys, preferred_element_type=jnp.f...  30.9 us
    another operation x4, loops' own time, head_pass(): return lax.map(query_pass, (head_queries, block_range))  21 us
    dynamic_slice x20, local copies, waits for them, and re-layouts, body(): lax.map(head_pass, jnp.arange(group_size, dtype=jnp.int32))  12.1 us
    reduce_sum x32, other arithmetic, block_attend(): row_total = jnp.sum(vert_exp, axis=(1, 2)) + jnp.sum(slash_exp, axis=(1, 2))  10.5 us
    gather x16, local copies, waits for them, and re-layouts, query_pass(): slash_blocks = jnp.take(head_reach, slash_index, axis=0)  9.56 us
  transfers between devices with their start and end apart: 6, of which 3 were waited for; matrix products, arithmetic and copies ran while one was open for 3% of the time, Pallas kernels for 0%

commit v1 on v0

--- a/solution.py
+++ b/solution.py
@@ -9,6 +9,12 @@
 BLOCK = 64
 NS = 8
 REACH = 2
+
+
+def _assign_words(buf, dimension_no):
+    work_now = list(buf.shape[1:])
+    work_now[dimension_no] *= buf.shape[0]
+    return jnp.moveaxis(buf, 0, dimension_no).reshape(work_now)
 
 
 def from_behind(value, axis, steps):
@@ -87,7 +93,25 @@
     my_heads = lax.dynamic_slice_in_dim(head_slot, group_rank * group_size, group_size)
     q_grouped = jnp.take(queries.reshape(tok_rows, H, DH), head_slot, axis=1)
     my_queries = lax.all_to_all(q_grouped, "head", split_axis=1, concat_axis=0, tiled=True)
-    whole_pairs = lax.all_gather(key_values, "head", axis=0, tiled=True)
+    shelf = []
+    n_lanes = lax.psum(1, "head")
+    for num in range(n_lanes):
+        shelf.append((num, (num + 1) % n_lanes))
+    frames = []
+    for k0, b in shelf:
+        frames.append((b, k0))
+    carry_out, main = ([], [])
+    for rr in range(n_lanes - 1):
+        if rr % 2 == 0:
+            carry_out.append(
+                lax.ppermute(carry_out[-1] if carry_out else key_values, "head", shelf)
+            )
+        else:
+            main.append(lax.ppermute(main[-1] if main else key_values, "head", frames))
+    kept_arr = jnp.stack([*carry_out[::-1], key_values, *main], 0)
+    val2 = lax.axis_index("head") - len(carry_out)
+    kept_arr = kept_arr[(jnp.arange(n_lanes) - val2) % n_lanes]
+    whole_pairs = _assign_words(kept_arr, 0)
     my_kv = lax.dynamic_slice_in_dim(kv_index, group_rank * group_size, group_size)
     my_pairs = jnp.take(whole_pairs.reshape(tok_dev, 2, KVH, DH), my_kv, axis=2)
     earlier = []

time: 334 us -> 315 us (0.943)
  waiting for transfers between devices: 99.8 us -> 72.1 us
  starting transfers between devices: 16.3 us -> 34.7 us
  blocking collectives: 45.2 us -> 34.8 us
    all_gather x1 -> x0, waiting for transfers between devices: 32.1 us -> none  [body(): whole_pairs = lax.all_gather(key_values, 'head', axis=0, tiled=True)]
    ppermute x0 -> x7, starting transfers between devices: none -> 16.3 us  [the longest x3 13.1 us: body(): main.append(lax.ppermute(main[-1] if main else key_values, 'head', frames))]
    unnamed x1, blocking collectives: 45.2 us -> 34.8 us
    ppermute x0 -> x7, waiting for transfers between devices: none -> 5.41 us  [the longest x4 5.3 us: body(): lax.ppermute(carry_out[-1] if carry_out else key_values, 'head', shelf)]
    all_to_all x1, starting transfers between devices: 3.6 us -> 8.63 us  [body(): lax.all_to_all(q_grouped, 'head', split_axis=1, concat_axis=0, tiled=True)]
  transfers between devices with their start and end apart: 6 -> 12, of which waited for: 3 -> 6; matrix products, arithmetic and copies ran while one was open for 3% -> 4% of each run, Pallas kernels for 0% -> 0%
where the time goes in v1:
time: 315 us; the launch traced here: 312 us
  waiting for transfers between devices  72.1 us (23%)
  local copies, waits for them, and re-layouts  59.8 us (19%)
  matrix products  47.1 us (15%)
  blocking collectives  34.8 us (11%)
  starting transfers between devices  34.7 us (11%)
  loops' own time  26.6 us (8%)
  other arithmetic  23 us (7%)
  between operations  14.2 us (5%)
    all_gather x1, waiting for transfers between devices, body(): lax.all_gather(packed[None], 'seq', axis=0, tiled=True)  60.2 us
    unnamed x1, blocking collectives  34.8 us
    dot_general x16, matrix products, block_attend(): jnp.einsum('qd,skd->qsk', q_rows, vert_keys, preferred_element_type=jnp.f...  30.9 us
    another operation x4, loops' own time, head_pass(): return lax.map(query_pass, (head_queries, block_range))  19.5 us
    ppermute x3, starting transfers between devices, body(): main.append(lax.ppermute(main[-1] if main else key_values, 'head', frames))  13.1 us
    dynamic_slice x20, local copies, waits for them, and re-layouts, body(): lax.map(head_pass, jnp.arange(group_size, dtype=jnp.int32))  11.7 us
    reduce_sum x32, other arithmetic, block_attend(): row_total = jnp.sum(vert_exp, axis=(1, 2)) + jnp.sum(slash_exp, axis=(1, 2))  10.5 us
    gather x16, local copies, waits for them, and re-layouts, query_pass(): slash_blocks = jnp.take(head_reach, slash_index, axis=0)  9.56 us
  transfers between devices with their start and end apart: 12, of which 6 were waited for; matrix products, arithmetic and copies ran while one was open for 4% of the time, Pallas kernels for 0%

profile of v1, /device:TPU:1, one launch (start us, length us, event | category | flops | bytes accessed | tf_op | source)
XLA Modules:
  0.0 312.3 jit_solution(17292299135536335317)
XLA Ops:
  6.5 2.6 collective-permute-start
  9.1 4.3 %collective-permute-start.4 = (bf16[32,2,1024]{2,1,0:T(2,128)(2,1)}, bf16[32,2,1024]{2,1,0:T(2,128)(2,1)S(1)}, u32[]{:S(2)}, u32[]{:S(2)}) collective-permute-start(bf16[32,2,1024]{2,1,0:T(2,128)(2,1)} %param.11), channel_id=1, source_target_pairs={{1,0},{2,1},{3,2},{4,3},{5,4},{6,5},{7,6},{0,7},{9,8},{10,9},{11,1... | collective-permute-start | bytes 393224 | tf_op jit(solution)/shard_map/ppermute | solution.py:110
  13.4 0.7 iota_add_fusion
  14.1 1.6 sort.17
  15.7 0.7 gather_fusion.1
  16.5 0.8 copy.62
  18.3 3.8 %collective-permute-done.1 = bf16[32,2,1024]{2,1,0:T(2,128)(2,1)S(1)} collective-permute-done((bf16[32,2,1024]{2,1,0:T(2,128)(2,1)S(1)}, bf16[32,2,1024]{2,1,0:T(2,128)(2,1)S(1)}, u32[]{:S(2)}, u32[]{:S(2)}) %collective-permute-start.1) | collective-permute-done | bytes 131104 | tf_op jit(solution)/shard_map/ppermute | solution.py:107
  22.7 4.2 %collective-permute-start.5 = (bf16[32,2,1024]{2,1,0:T(2,128)(2,1)S(1)}, bf16[32,2,1024]{2,1,0:T(2,128)(2,1)S(1)}, u32[]{:S(2)}, u32[]{:S(2)}) collective-permute-start(bf16[32,2,1024]{2,1,0:T(2,128)(2,1)S(1)} %collective-permute-done.4), channel_id=1, source_target_pairs={{1,0},{2,1},{3,2},{4,3},{5,4},{6,5},{7,6},{0,7},{9,8},{10,9},{11,1... | collective-permute-start | bytes 393224 | tf_op jit(solution)/shard_map/ppermute | solution.py:110
  26.9 0.8 collective-permute-done.2
  27.8 4.7 %collective-permute-start.6 = (bf16[32,2,1024]{2,1,0:T(2,128)(2,1)S(1)}, bf16[32,2,1024]{2,1,0:T(2,128)(2,1)S(1)}, u32[]{:S(2)}, u32[]{:S(2)}) collective-permute-start(bf16[32,2,1024]{2,1,0:T(2,128)(2,1)S(1)} %collective-permute-done.5), channel_id=1, source_target_pairs={{1,0},{2,1},{3,2},{4,3},{5,4},{6,5},{7,6},{0,7},{9,8},{10,9},{11,1... | collective-permute-start | bytes 393224 | tf_op jit(solution)/shard_map/ppermute | solution.py:110
  32.5 0.7 collective-permute-done.3
  33.7 1.0 bitcast_dynamic-update-slice_fusion.4
  35.0 2.7 gather_fusion.4
  37.7 0.7 reshape.411
  38.7 0.6 gather_fusion.5
  40.0 0.7 copy.99
  41.5 1.3 collective-permute-start.7
  42.8 3.2 %collective-permute-start.8 = (bf16[256,2,4,128]{3,0,1,2:T(8,128)(2,1)S(1)}, bf16[256,2,4,128]{3,0,1,2:T(8,128)(2,1)S(1)}, u32[]{:S(2)}, u32[]{:S(2)}) collective-permute-start(bf16[256,2,4,128]{3,0,1,2:T(8,128)(2,1)S(1)} %bitcast_select_fusion), channel_id=1, source_target_pairs={{0,8},{8,16},{16,24},{24,32},{32,40},{40,48},{48,56},{56,64},{64,7... | collective-permute-start | bytes 1572872 | tf_op jit(solution)/shard_map/ppermute | solution.py:23
  46.0 0.8 select_bitcast_fusion
  46.9 8.6 %all-to-all-start = ((bf16[32,32,128]{2,0,1:T(8,128)(2,1)}), bf16[32,32,128]{2,0,1:T(8,128)(2,1)S(1)}, u32[]{:S(2)}, u32[]{:S(2)}) async-start(bf16[32,32,128]{2,0,1:T(8,128)(2,1)} %select_bitcast_fusion), calls=%async_computation | async-start | bytes 524288 | tf_op jit(solution)/shard_map/all_to_all | solution.py:95
  56.2 1.3 dynamic-slice
  58.3 34.8 %all-reduce = s32[256]{0:T(256)S(1)} all-reduce(s32[256]{0:T(256)S(1)} %dynamic-update-slice), channel_id=3, replica_groups=mesh['seq'=64,'head'=8] {'seq'}, use_global_device_ids=true, to_apply=%add | all-reduce | flops 256 | bytes 2048
  94.0 1.3 pad_maximum_fusion
  95.4 60.2 %all-gather.4.cloned.1.call-done = bf16[256,2,64,128]{3,2,1,0:T(8,128)(2,1)} async-done(((bf16[4,2,64,128]{3,2,1,0:T(8,128)(2,1)}), bf16[256,2,64,128]{3,2,1,0:T(8,128)(2,1)}) %all-gather.4.cloned.1.call-update) | async-done | bytes 8388624 | tf_op jit(solution)/shard_map/all_gather | solution.py:135
  155.6 134.7 %while.37 = (s32[]{:T(128)}, bf16[4,4,64,128]{3,2,1,0:T(8,128)(2,1)}, s32[4]{0:T(128)S(1)}, bf16[256,4,128]{2,0,1:T(8,128)(2,1)S(1)}, s32[4,8]{1,0:T(4,128)S(1)}...) while((s32[]{:T(128)}, ...), condition=%wide.region_11.12_spmd.clone.clone, body=%wide.region_3.11_spmd.clone.clone.sunk | while | flops 154098576 | bytes 21907556 | solution.py:179
  157.9 1.8 copy_bitcast_fusion.6
  159.7 1.5 slice_bitcast_fusion.8
  161.2 1.0 copy_bitcast_fusion.7
  163.4 25.2 %while.38 = (s32[]{:T(128)}, bf16[4,64,128]{2,1,0:T(8,128)(2,1)S(1)}, s32[64]{0:T(128)S(1)}, s32[4]{0:T(128)S(1)}, s32[]{:T(128)}, /*index=5*/s32[8]{0:T(128)S(1...) while((s32[]{:T(128)}, ...), condition=%wide.region_10.10_spmd, body=%wide.region_4.9_spmd.sunk | while | flops 154098560 | bytes 12468941 | solution.py:177
  164.7 1.9 fusion.58
  171.0 1.9 fusion.58
  177.3 1.9 fusion.58
  183.6 1.9 fusion.58
  188.6 0.6 bitcast_dynamic-update-slice_fusion.10
  191.6 1.8 copy_bitcast_fusion.6
  193.4 1.5 slice_bitcast_fusion.8
  194.9 1.0 copy_bitcast_fusion.7
  197.1 25.2 %while.38 = (s32[]{:T(128)}, bf16[4,64,128]{2,1,0:T(8,128)(2,1)S(1)}, s32[64]{0:T(128)S(1)}, s32[4]{0:T(128)S(1)}, s32[]{:T(128)}, /*index=5*/s32[8]{0:T(128)S(1...) while((s32[]{:T(128)}, ...), condition=%wide.region_10.10_spmd, body=%wide.region_4.9_spmd.sunk | while | flops 154098560 | bytes 12468941 | solution.py:177
  198.4 1.9 fusion.58
  204.7 1.9 fusion.58
  211.0 1.9 fusion.58
  217.3 1.9 fusion.58
  222.3 0.6 bitcast_dynamic-update-slice_fusion.10
  225.3 1.8 copy_bitcast_fusion.6
  227.0 1.5 slice_bitcast_fusion.8
  228.5 1.0 copy_bitcast_fusion.7
  230.8 25.2 %while.38 = (s32[]{:T(128)}, bf16[4,64,128]{2,1,0:T(8,128)(2,1)S(1)}, s32[64]{0:T(128)S(1)}, s32[4]{0:T(128)S(1)}, s32[]{:T(128)}, /*index=5*/s32[8]{0:T(128)S(1...) while((s32[]{:T(128)}, ...), condition=%wide.region_10.10_spmd, body=%wide.region_4.9_spmd.sunk | while | flops 154098560 | bytes 12468941 | solution.py:177
  232.1 1.9 fusion.58
  238.4 1.9 fusion.58
  244.7 1.9 fusion.58
  251.0 1.9 fusion.58
  256.0 0.6 bitcast_dynamic-update-slice_fusion.10
  258.9 1.8 copy_bitcast_fusion.6
  260.7 1.5 slice_bitcast_fusion.8
  262.2 1.0 copy_bitcast_fusion.7
  264.5 25.2 %while.38 = (s32[]{:T(128)}, bf16[4,64,128]{2,1,0:T(8,128)(2,1)S(1)}, s32[64]{0:T(128)S(1)}, s32[4]{0:T(128)S(1)}, s32[]{:T(128)}, /*index=5*/s32[8]{0:T(128)S(1...) while((s32[]{:T(128)}, ...), condition=%wide.region_10.10_spmd, body=%wide.region_4.9_spmd.sunk | while | flops 154098560 | bytes 12468941 | solution.py:177
  265.8 1.9 fusion.58
  272.1 1.9 fusion.58
  278.4 1.9 fusion.58
  284.7 1.9 fusion.58
  290.3 1.9 copy.66
  292.2 5.2 %all-to-all-start.1 = ((bf16[4,256,128]{2,0,1:T(4,128)(2,1)}), bf16[4,256,128]{2,0,1:T(4,128)(2,1)S(1)}, u32[]{:S(2)}, u32[]{:S(2)}) async-start(bf16[4,256,128]{2,0,1:T(4,128)(2,1)} %bitcast.34), calls=%async_computation.1 | async-start | bytes 524288 | tf_op jit(solution)/shard_map/all_to_all | solution.py:182
  297.4 6.5 %all-to-all-done.1 = bf16[4,256,128]{2,0,1:T(4,128)(2,1)S(1)} async-done(((bf16[4,256,128]{2,0,1:T(4,128)(2,1)}), bf16[4,256,128]{2,0,1:T(4,128)(2,1)S(1)}, u32[]{:S(2)}, u32[]{:S(2)}) %all-to-all-start.1) | async-done | bytes 262176 | tf_op jit(solution)/shard_map/all_to_all | solution.py:182
  304.6 0.9 copy_bitcast_fusion.2
  (401 shorter events, 64.9 us)
Async XLA Ops:
  6.5 34.2 %copy-start = (bf16[32,4096]{1,0:T(8,128)(2,1)S(1)}, bf16[32,4096]{1,0:T(8,128)(2,1)}, u32[]{:S(2)}) copy-start(bf16[32,4096]{1,0:T(8,128)(2,1)} %param.10) | copy-start | bytes 786436
  6.5 149.0 %all-gather.4.cloned.1.call-start = ((), (), s32[]{:S(2)}) async-start(), calls=%async_computation.2 | async-start | bytes 8519680 | tf_op jit(solution)/shard_map/all_gather | solution.py:135
  6.5 11.7 %collective-permute-start = (bf16[32,2,1024]{2,1,0:T(2,128)(2,1)}, bf16[32,2,1024]{2,1,0:T(2,128)(2,1)S(1)}, u32[]{:S(2)}, u32[]{:S(2)}) collective-permute-start(bf16[32,2,1024]{2,1,0:T(2,128)(2,1)} %param.11), channel_id=1, source_target_pairs={{0,1},{1,2},{2,3},{3,4},{4,5},{5,6},{6,7},{7,0},{8,9},{9,10},{10,1... | collective-permute-start | bytes 393224 | tf_op jit(solution)/shard_map/ppermute | solution.py:107
  9.1 13.5 %collective-permute-start.4 = (bf16[32,2,1024]{2,1,0:T(2,128)(2,1)}, bf16[32,2,1024]{2,1,0:T(2,128)(2,1)S(1)}, u32[]{:S(2)}, u32[]{:S(2)}) collective-permute-start(bf16[32,2,1024]{2,1,0:T(2,128)(2,1)} %param.11), channel_id=1, source_target_pairs={{1,0},{2,1},{3,2},{4,3},{5,4},{6,5},{7,6},{0,7},{9,8},{10,9},{11,1... | collective-permute-start | bytes 393224 | tf_op jit(solution)/shard_map/ppermute | solution.py:110
  18.2 3.8 %collective-permute-start.1 = (bf16[32,2,1024]{2,1,0:T(2,128)(2,1)S(1)}, bf16[32,2,1024]{2,1,0:T(2,128)(2,1)S(1)}, u32[]{:S(2)}, u32[]{:S(2)}) collective-permute-start(bf16[32,2,1024]{2,1,0:T(2,128)(2,1)S(1)} %collective-permute-done), channel_id=1, source_target_pairs={{0,1},{1,2},{2,3},{3,4},{4,5},{5,6},{6,7},{7,0},{8,9},{9,10},{10,1... | collective-permute-start | bytes 393224 | tf_op jit(solution)/shard_map/ppermute | solution.py:107
  22.0 5.6 %collective-permute-start.2 = (bf16[32,2,1024]{2,1,0:T(2,128)(2,1)S(1)}, bf16[32,2,1024]{2,1,0:T(2,128)(2,1)S(1)}, u32[]{:S(2)}, u32[]{:S(2)}) collective-permute-start(bf16[32,2,1024]{2,1,0:T(2,128)(2,1)S(1)} %collective-permute-done.1), channel_id=1, source_target_pairs={{0,1},{1,2},{2,3},{3,4},{4,5},{5,6},{6,7},{7,0},{8,9},{9,10},{10,1... | collective-permute-start | bytes 393224 | tf_op jit(solution)/shard_map/ppermute | solution.py:107
  22.7 5.2 %collective-permute-start.5 = (bf16[32,2,1024]{2,1,0:T(2,128)(2,1)S(1)}, bf16[32,2,1024]{2,1,0:T(2,128)(2,1)S(1)}, u32[]{:S(2)}, u32[]{:S(2)}) collective-permute-start(bf16[32,2,1024]{2,1,0:T(2,128)(2,1)S(1)} %collective-permute-done.4), channel_id=1, source_target_pairs={{1,0},{2,1},{3,2},{4,3},{5,4},{6,5},{7,6},{0,7},{9,8},{10,9},{11,1... | collective-permute-start | bytes 393224 | tf_op jit(solution)/shard_map/ppermute | solution.py:110
  27.7 5.6 %collective-permute-start.3 = (bf16[32,2,1024]{2,1,0:T(2,128)(2,1)S(1)}, bf16[32,2,1024]{2,1,0:T(2,128)(2,1)S(1)}, u32[]{:S(2)}, u32[]{:S(2)}) collective-permute-start(bf16[32,2,1024]{2,1,0:T(2,128)(2,1)S(1)} %collective-permute-done.2), channel_id=1, source_target_pairs={{0,1},{1,2},{2,3},{3,4},{4,5},{5,6},{6,7},{7,0},{8,9},{9,10},{10,1... | collective-permute-start | bytes 393224 | tf_op jit(solution)/shard_map/ppermute | solution.py:107
  27.8 7.1 %collective-permute-start.6 = (bf16[32,2,1024]{2,1,0:T(2,128)(2,1)S(1)}, bf16[32,2,1024]{2,1,0:T(2,128)(2,1)S(1)}, u32[]{:S(2)}, u32[]{:S(2)}) collective-permute-start(bf16[32,2,1024]{2,1,0:T(2,128)(2,1)S(1)} %collective-permute-done.5), channel_id=1, source_target_pairs={{1,0},{2,1},{3,2},{4,3},{5,4},{6,5},{7,6},{0,7},{9,8},{10,9},{11,1... | collective-permute-start | bytes 393224 | tf_op jit(solution)/shard_map/ppermute | solution.py:110
  40.0 15.5 %copy-start.1 = (s32[32]{0:T(128)S(1)}, s32[32]{0:T(128)}, u32[]{:S(2)}) copy-start(s32[32]{0:T(128)} %param.15) | copy-start | bytes 388
  40.0 53.3 %copy-start.4 = (s32[32,8]{0,1:T(8,128)S(1)}, s32[32,8]{0,1:T(8,128)}, u32[]{:S(2)}) copy-start(s32[32,8]{0,1:T(8,128)} %param.14) | copy-start | bytes 3076
  41.5 52.5 %collective-permute-start.7 = (bf16[256,2,4,128]{3,0,1,2:T(8,128)(2,1)S(1)}, bf16[256,2,4,128]{3,0,1,2:T(8,128)(2,1)S(1)}, u32[]{:S(2)}, u32[]{:S(2)}) collective-permute-start(bf16[256,2,4,128]{3,0,1,2:T(8,128)(2,1)S(1)} %bitcast_select_fusion), channel_id=1, source_target_pairs={{0,16},{8,24},{16,32},{24,40},{32,48},{40,56},{48,64},{56,72},{64,... | collective-permute-start | bytes 1572872 | tf_op jit(solution)/shard_map/ppermute | solution.py:23
  42.8 51.2 %collective-permute-start.8 = (bf16[256,2,4,128]{3,0,1,2:T(8,128)(2,1)S(1)}, bf16[256,2,4,128]{3,0,1,2:T(8,128)(2,1)S(1)}, u32[]{:S(2)}, u32[]{:S(2)}) collective-permute-start(bf16[256,2,4,128]{3,0,1,2:T(8,128)(2,1)S(1)} %bitcast_select_fusion), channel_id=1, source_target_pairs={{0,8},{8,16},{16,24},{24,32},{32,40},{40,48},{48,56},{56,64},{64,7... | collective-permute-start | bytes 1572872 | tf_op jit(solution)/shard_map/ppermute | solution.py:23
  46.9 47.1 %all-to-all-start = ((bf16[32,32,128]{2,0,1:T(8,128)(2,1)}), bf16[32,32,128]{2,0,1:T(8,128)(2,1)S(1)}, u32[]{:S(2)}, u32[]{:S(2)}) async-start(bf16[32,32,128]{2,0,1:T(8,128)(2,1)} %select_bitcast_fusion), calls=%async_computation | async-start | bytes 524288 | tf_op jit(solution)/shard_map/all_to_all | solution.py:95
  168.0 1.2 copy-start.2
  174.3 1.2 copy-start.2
  180.6 1.2 copy-start.2
  186.9 1.2 copy-start.2
  201.7 1.2 copy-start.2
  207.9 1.2 copy-start.2
  214.2 1.2 copy-start.2
  220.5 1.2 copy-start.2
  235.3 1.2 copy-start.2
  241.6 1.2 copy-start.2
  247.9 1.2 copy-start.2
  254.2 1.2 copy-start.2
  269.0 1.2 copy-start.2
  275.3 1.2 copy-start.2
  281.6 1.2 copy-start.2
  287.9 1.2 copy-start.2
  290.3 14.2 %copy-start.3 = (bf16[32,4096]{1,0:T(8,128)(2,1)S(1)}, bf16[32,4096]{1,0:T(8,128)(2,1)}, u32[]{:S(2)}) copy-start(bf16[32,4096]{1,0:T(8,128)(2,1)} %param.12) | copy-start | bytes 786436
  292.2 11.7 %all-to-all-start.1 = ((bf16[4,256,128]{2,0,1:T(4,128)(2,1)}), bf16[4,256,128]{2,0,1:T(4,128)(2,1)S(1)}, u32[]{:S(2)}, u32[]{:S(2)}) async-start(bf16[4,256,128]{2,0,1:T(4,128)(2,1)} %bitcast.34), calls=%async_computation.1 | async-start | bytes 524288 | tf_op jit(solution)/shard_map/all_to_all | solution.py:182
Sparse Core Ops, SparseCore 0:
  40.8 114.7 all-gather.3
